TPU v7x, 128 devices: a whole 4x4x4 slice. The times are simulated.
128 devices in a mesh: row: 16 (over x, z), col: 8 (over y, core).
Axes of the slice: x: 4, y: 4, z: 4, core: 2. Of those that a mesh axis runs over, the one named last changes fastest.
Arguments:
- primal_rows: bfloat16 [16384, 8192], P('row', 'col'), may hold values from -6 to 6
- dual_rows: bfloat16 [16384, 8192], P('row', 'col'), may hold values from -6 to 6
- weight_rows: bfloat16 [16384, 8192], P('row', 'col'), may hold values from -0.0625 to 0.0625
- pairs: int32 [384, 2], P('row'), may hold values from 0 to 63, as said below
Outputs:
- tiles: float32 [384, 256, 256], P('row', 'col')
Inputs may be any that keep to these rules, and one draw needn't show every extreme that they name: `pairs`: tile rows r * 24 to (r + 1) * 24 - 1 have their first block i among blocks r * 4 to (r + 1) * 4 - 1. Among their second blocks j, the blocks held by any other row index q (blocks q * 4 to (q + 1) * 4 - 1) are exactly one block, named one or more times; blocks of r itself may appear too.
All inputs are finite; a program needn't handle non-finite values.
Results may differ from a plain program's by a relative error of at most 0.0003.
Values may be sent and summed in bfloat16 or wider, within the bound.
No kernel may reach another device: no remote copies, remote signals or barrier semaphores. Data moves between devices by JAX's collectives and lax.ppermute only.
A program may use at most 128 MiB of HBM per device.

v0:
```python
import jax
import jax.numpy as jnp
from jax import lax
from jax.sharding import PartitionSpec as P

TILE = 256


def shards(primal_rows, dual_rows, weight_rows, pairs):
    row_count = lax.axis_size("row")
    my_row = lax.axis_index("row")
    per_row = primal_rows.shape[0] // TILE
    features = primal_rows.shape[1]
    tile_count = pairs.shape[0]
    every_pair = lax.all_gather(pairs, "row", axis=0, tiled=True)
    wanted = every_pair.reshape(row_count, tile_count * 2)
    held_here = wanted // per_row == my_row
    local_pick = jnp.max(jnp.where(held_here, wanted - my_row * per_row, 0), axis=1)
    weight_blocks = weight_rows.reshape(per_row, TILE, features)
    outgoing = jnp.take(weight_blocks, local_pick, axis=0)
    incoming = lax.all_to_all(outgoing, "row", split_axis=0, concat_axis=0, tiled=True)
    block_table = jnp.concatenate([weight_blocks, incoming], axis=0)
    first_local = pairs[:, 0] - my_row * per_row
    second_block = pairs[:, 1]
    second_row = second_block // per_row
    second_slot = jnp.where(
        second_row == my_row, second_block - my_row * per_row, per_row + second_row
    )
    left_x = jnp.take(primal_rows.reshape(per_row, TILE, features), first_local, axis=0)
    left_s = jnp.take(dual_rows.reshape(per_row, TILE, features), first_local, axis=0)
    right_rows = jnp.take(block_table, second_slot, axis=0)
    cross_x = jnp.einsum("tak,tbk->tab", left_x, right_rows, preferred_element_type=jnp.float32)
    cross_s = jnp.einsum("tak,tbk->tab", left_s, right_rows, preferred_element_type=jnp.float32)
    stacked = jnp.stack([cross_x, cross_s])
    whole = lax.psum(stacked, "col")
    slice_rows = TILE // lax.axis_size("col")
    summed = lax.dynamic_slice_in_dim(whole, lax.axis_index("col") * slice_rows, slice_rows, 2)
    return summed[0] * summed[1]


def solution(mesh):
    placed = (P("row", "col"), P("row", "col"), P("row", "col"), P("row", None))
    return jax.shard_map(
        shards, mesh=mesh, in_specs=placed, out_specs=P("row", "col", None), check_vma=False
    )
```

profile of v0, /device:TPU:1, one launch (start us, length us, event | category | flops | bytes accessed | tf_op | source)
XLA Modules:
  0.0 358.9 jit_solution(2798819045864562003)
XLA Ops:
  6.5 0.0 copy-start
  6.5 20.3 %all-gather = s32[16,24,2]{1,2,0:T(2,128)S(1)} all-gather(s32[1,24,2]{1,2,0:T(2,128)} %bitcast.26), channel_id=1, replica_groups=mesh['row'=16,'col'=8] {'row'}, dimensions={0}, use_global_device_ids=true | all-gather | bytes 3264 | tf_op jit(solution)/shard_map/all_gather | solution.py:15
  26.8 0.1 reshape.79
  27.0 0.1 reduce_max.15
  27.0 0.1 reduce_max.20
  27.2 6.2 %gather_fusion = bf16[16,256,1024]{2,1,0:T(8,128)(2,1)} fusion(bf16[4,256,1024]{2,1,0:T(8,128)(2,1)} %bitcast.24, s32[1024]{0:T(1024)S(1)} %pad_clamp_fusion.1), kind=kCustom, calls=%fused_computation.2 | custom fusion | bytes 16777280 | tf_op jit(solution)/shard_map/jit(_take)/gather | solution.py:20
  33.4 7.4 %broadcast_select_fusion.1 = bf16[16,256,1024]{2,1,0:T(8,128)(2,1)} fusion(bf16[16,256,1024]{2,1,0:T(8,128)(2,1)} %gather_fusion, pred[16]{0:T(512)(128)(4,1)S(1)} %compare_and_fusion.1), kind=kLoop, calls=%fused_computation.13 | loop fusion | flops 4194304 | bytes 16777232 | tf_op jit(solution)/shard_map/jit(_take)/select_n | solution.py:20
  40.9 0.0 copy-start.3
  40.9 4.9 %all-to-all-start = ((bf16[16,256,1024]{2,1,0:T(8,128)(2,1)}), bf16[16,256,1024]{2,1,0:T(8,128)(2,1)}, u32[]{:S(2)}, u32[]{:S(2)}) async-start(bf16[16,256,1024]{2,1,0:T(8,128)(2,1)} %broadcast_select_fusion.1), calls=%async_computation | async-start | bytes 16777216 | tf_op jit(solution)/shard_map/all_to_all | solution.py:21
  45.8 0.0 all-reduce.2.cloned.1.call-start
  45.9 0.0 copy-done.3
  45.9 0.0 copy-done
  45.9 6.0 %gather_fusion.2 = bf16[24,256,1024]{2,1,0:T(8,128)(2,1)} fusion(bf16[4,256,1024]{2,1,0:T(8,128)(2,1)S(1)} %bitcast.22, s32[1024]{0:T(1024)S(1)} %pad_clamp_fusion.2), kind=kCustom, calls=%fused_computation.clone | custom fusion | bytes 25165920 | tf_op jit(solution)/shard_map/jit(_take)/gather | solution.py:29
  51.9 0.0 copy-start.2
  51.9 7.8 %gather_fusion.3 = bf16[24,256,1024]{2,1,0:T(8,128)(2,1)} fusion(bf16[4,256,1024]{2,1,0:T(8,128)(2,1)} %bitcast.23, s32[1024]{0:T(1024)S(1)} %pad_clamp_fusion.2), kind=kCustom, calls=%fused_computation.1.clone | custom fusion | bytes 25165920 | tf_op jit(solution)/shard_map/jit(_take)/gather | solution.py:30
  59.7 83.6 %all-to-all-done = bf16[16,256,1024]{2,1,0:T(8,128)(2,1)} async-done(((bf16[16,256,1024]{2,1,0:T(8,128)(2,1)}), bf16[16,256,1024]{2,1,0:T(8,128)(2,1)}, u32[]{:S(2)}, u32[]{:S(2)}) %all-to-all-start) | async-done | bytes 8388640 | tf_op jit(solution)/shard_map/all_to_all | solution.py:21
  143.4 0.0 copy-done.2
  143.4 8.6 %pad_maximum_fusion.1 = bf16[20,256,1024]{2,1,0:T(8,128)(2,1)} fusion(bf16[16,256,1024]{2,1,0:T(8,128)(2,1)} %all-to-all-done, bf16[4,256,1024]{2,1,0:T(8,128)(2,1)S(1)} %bitcast.25), kind=kLoop, calls=%fused_computation.12 | loop fusion | flops 5242880 | bytes 20971520 | tf_op jit(solution)/shard_map/concatenate | solution.py:22
  152.0 10.1 %gather_fusion.1 = bf16[24,256,1024]{2,1,0:T(8,128)(2,1)} fusion(bf16[20,256,1024]{2,1,0:T(8,128)(2,1)} %pad_maximum_fusion.1, s32[1024]{0:T(1024)S(1)} %pad_clamp_fusion), kind=kCustom, calls=%fused_computation.3 | custom fusion | bytes 25165920 | tf_op jit(solution)/shard_map/jit(_take)/gather | solution.py:31
  162.1 13.1 %fusion.8 = f32[1,24,256,256]{3,2,1,0:T(8,128)} fusion(bf16[24,256,1024]{2,1,0:T(8,128)(2,1)} %gather_fusion.1, pred[24]{0:T(512)(128)(4,1)S(1)} %get-tuple-element.8, bf16[24,256,1024]{2,1,0:T(8,128)(2,1)} %gather_fusion.2, pred[24]{0:T(512)(128)(4,1)S(1)} %get-tuple-element.6), kind=kOutput, calls=%fused_computation.16 | convolution fusion | flops 3233808384 | bytes 31457328 | tf_op jit(solution)/shard_map/tak,tbk->tab/dot_general | solution.py:32
  175.1 13.0 %fusion.11 = f32[1,24,256,256]{3,2,1,0:T(8,128)} fusion(bf16[24,256,1024]{2,1,0:T(8,128)(2,1)} %gather_fusion.1, pred[24]{0:T(512)(128)(4,1)S(1)} %get-tuple-element.8, bf16[24,256,1024]{2,1,0:T(8,128)(2,1)} %gather_fusion.3, pred[24]{0:T(512)(128)(4,1)S(1)} %get-tuple-element.6), kind=kOutput, calls=%fused_computation.17 | convolution fusion | flops 3233808384 | bytes 31457328 | tf_op jit(solution)/shard_map/tak,tbk->tab/dot_general | solution.py:33
  188.2 0.0 copy-start.1
  188.2 10.7 %pad_maximum_fusion = f32[2,24,256,256]{3,2,1,0:T(8,128)} fusion(f32[1,24,256,256]{3,2,1,0:T(8,128)} %fusion.11, f32[1,24,256,256]{3,2,1,0:T(8,128)} %fusion.8), kind=kLoop, calls=%fused_computation.4 | loop fusion | flops 3145728 | bytes 25165824 | tf_op jit(solution)/shard_map/stack | solution.py:34
  198.9 0.0 all-reduce.2.cloned.1.call-update
  198.9 150.7 %all-reduce.2.cloned.1.call-done = f32[2,24,256,256]{3,2,1,0:T(8,128)} async-done(((f32[2,24,256,256]{3,2,1,0:T(8,128)}), f32[2,24,256,256]{3,2,1,0:T(8,128)}) %all-reduce.2.cloned.1.call-update) | async-done | bytes 12582928 | tf_op jit(solution)/shard_map/psum | solution.py:35
  349.6 2.4 fusion.14
  352.0 0.0 copy-done.1
  (9 shorter events, 0.1 us)
Async XLA Ops:
  6.5 39.4 %copy-start = (bf16[1024,1024]{1,0:T(8,128)(2,1)S(1)}, bf16[1024,1024]{1,0:T(8,128)(2,1)}, u32[]{:S(2)}) copy-start(bf16[1024,1024]{1,0:T(8,128)(2,1)} %param.6) | copy-start | bytes 6291460
  40.9 5.0 %copy-start.3 = (s32[24,2]{0,1:T(2,128)S(1)}, s32[24,2]{0,1:T(2,128)}, u32[]{:S(2)}) copy-start(s32[24,2]{0,1:T(2,128)} %param.9) | copy-start | bytes 580
  40.9 102.5 %all-to-all-start = ((bf16[16,256,1024]{2,1,0:T(8,128)(2,1)}), bf16[16,256,1024]{2,1,0:T(8,128)(2,1)}, u32[]{:S(2)}, u32[]{:S(2)}) async-start(bf16[16,256,1024]{2,1,0:T(8,128)(2,1)} %broadcast_select_fusion.1), calls=%async_computation | async-start | bytes 16777216 | tf_op jit(solution)/shard_map/all_to_all | solution.py:21
  45.8 303.8 %all-reduce.2.cloned.1.call-start = ((), (), s32[]{:S(2)}) async-start(), calls=%async_computation.1 | async-start | bytes 25165824 | tf_op jit(solution)/shard_map/psum | solution.py:35
  51.9 91.5 %copy-start.2 = (bf16[1024,1024]{1,0:T(8,128)(2,1)S(1)}, bf16[1024,1024]{1,0:T(8,128)(2,1)}, u32[]{:S(2)}) copy-start(bf16[1024,1024]{1,0:T(8,128)(2,1)} %param.8) | copy-start | bytes 6291460
  188.2 163.8 %copy-start.1 = (bf16[1024,1024]{1,0:T(8,128)(2,1)S(1)}, bf16[1024,1024]{1,0:T(8,128)(2,1)}, u32[]{:S(2)}) copy-start(bf16[1024,1024]{1,0:T(8,128)(2,1)} %param.6) | copy-start | bytes 6291460
Sparse Core Ops, SparseCore 0:
  199.1 150.5 all-reduce.1
where the time goes:
time: 359 us
  waiting for transfers between devices  234 us (65%)
  local copies, waits for them, and re-layouts  30.3 us (8%)
  other arithmetic  29.4 us (8%)
  matrix products  26.1 us (7%)
  blocking collectives  20.3 us (6%)
  between operations  13.5 us (4%)
  starting transfers between devices  4.98 us (1%)
    psum x1, waiting for transfers between devices, shards(): whole = lax.psum(stacked, 'col')  151 us
    all_to_all x1, waiting for transfers between devices, shards(): lax.all_to_all(outgoing, 'row', split_axis=0, concat_axis=0, tiled=True)  83.6 us
    all_gather x1, blocking collectives, shards(): every_pair = lax.all_gather(pairs, 'row', axis=0, tiled=True)  20.3 us
    dot_general x1, matrix products, shards(): jnp.einsum('tak,tbk->tab', left_x, right_rows, preferred_element_type=jnp...  13.1 us
    dot_general x1, matrix products, shards(): jnp.einsum('tak,tbk->tab', left_s, right_rows, preferred_element_type=jnp...  13 us
    another operation x1, other arithmetic, shards(): stacked = jnp.stack([cross_x, cross_s])  10.7 us
    gather x1, local copies, waits for them, and re-layouts, shards(): right_rows = jnp.take(block_table, second_slot, axis=0)  10.1 us
    concatenate x1, other arithmetic, shards(): block_table = jnp.concatenate([weight_blocks, incoming], axis=0)  8.62 us
  transfers between devices with their start and end apart: 2, of which 2 were waited for; matrix products, arithmetic and copies ran while one was open for 4% of the time, Pallas kernels for 0%

commit v1 on v0

--- a/solution.py
+++ b/solution.py
@@ -32,7 +32,7 @@
     cross_x = jnp.einsum("tak,tbk->tab", left_x, right_rows, preferred_element_type=jnp.float32)
     cross_s = jnp.einsum("tak,tbk->tab", left_s, right_rows, preferred_element_type=jnp.float32)
     stacked = jnp.stack([cross_x, cross_s])
-    whole = lax.psum(stacked, "col")
+    whole = jnp.sum(lax.all_gather(stacked, "col"), axis=0)
     slice_rows = TILE // lax.axis_size("col")
     summed = lax.dynamic_slice_in_dim(whole, lax.axis_index("col") * slice_rows, slice_rows, 2)
     return summed[0] * summed[1]

time: 359 us -> 690 us (1.92)
  waiting for transfers between devices: 234 us -> 529 us
  other arithmetic: 29.4 us -> 65.1 us
    all_gather x0 -> x1, waiting for transfers between devices: none -> 446 us  [shards(): whole = jnp.sum(lax.all_gather(stacked, 'col'), axis=0)]
    psum x1 -> x0, waiting for transfers between devices: 151 us -> none  [shards(): whole = lax.psum(stacked, 'col')]
    reduce_sum x0 -> x1, other arithmetic: none -> 35.9 us  [shards(): whole = jnp.sum(lax.all_gather(stacked, 'col'), axis=0)]
  transfers between devices with their start and end apart: 2 -> 2, of which waited for: 2 -> 2; matrix products, arithmetic and copies ran while one was open for 4% -> 2% of each run, Pallas kernels for 0% -> 0%
where the time goes in v1:
time: 690 us
  waiting for transfers between devices  529 us (77%)
  other arithmetic  65.1 us (9%)
  local copies, waits for them, and re-layouts  30.3 us (4%)
  matrix products  26.1 us (4%)
  blocking collectives  20.3 us (3%)
  between operations  13.5 us (2%)
    all_gather x1, waiting for transfers between devices, shards(): whole = jnp.sum(lax.all_gather(stacked, 'col'), axis=0)  446 us
    all_to_all x1, waiting for transfers between devices, shards(): lax.all_to_all(outgoing, 'row', split_axis=0, concat_axis=0, tiled=True)  83.6 us
    reduce_sum x1, other arithmetic, shards(): whole = jnp.sum(lax.all_gather(stacked, 'col'), axis=0)  35.9 us
    all_gather x1, blocking collectives, shards(): every_pair = lax.all_gather(pairs, 'row', axis=0, tiled=True)  20.3 us
  transfers between devices with their start and end apart: 2, of which 2 were waited for; matrix products, arithmetic and copies ran while one was open for 2% of the time, Pallas kernels for 0%

profile of v1, /device:TPU:1, one launch (start us, length us, event | category | flops | bytes accessed | tf_op | source)
XLA Modules:
  0.0 689.6 jit_solution(8684105692919679544)
XLA Ops:
  6.5 0.0 copy-start
  6.5 20.3 %all-gather.1 = s32[16,24,2]{1,2,0:T(2,128)S(1)} all-gather(s32[1,24,2]{1,2,0:T(2,128)} %bitcast.27), channel_id=1, replica_groups=mesh['row'=16,'col'=8] {'row'}, dimensions={0}, use_global_device_ids=true | all-gather | bytes 3264 | tf_op jit(solution)/shard_map/all_gather | solution.py:15
  26.8 0.1 reshape.80
  27.0 0.1 reduce_max.15
  27.0 0.1 reduce_max.20
  27.2 6.2 gather_fusion
  33.4 7.4 %broadcast_select_fusion.1 = bf16[16,256,1024]{2,1,0:T(8,128)(2,1)} fusion(bf16[16,256,1024]{2,1,0:T(8,128)(2,1)} %gather_fusion, pred[16]{0:T(512)(128)(4,1)S(1)} %compare_and_fusion.1), kind=kLoop, calls=%fused_computation.13 | loop fusion | flops 4194304 | bytes 16777232 | tf_op jit(solution)/shard_map/jit(_take)/select_n | solution.py:20
  40.9 0.0 copy-start.3
  40.9 4.9 all-to-all-start
  45.8 0.0 all-gather.4.cloned.1.call-start
  45.9 0.0 copy-done.3
  45.9 0.0 copy-done
  45.9 6.0 gather_fusion.2
  51.9 0.0 copy-start.2
  51.9 7.8 %gather_fusion.3 = bf16[24,256,1024]{2,1,0:T(8,128)(2,1)} fusion(bf16[4,256,1024]{2,1,0:T(8,128)(2,1)} %bitcast.24, s32[1024]{0:T(1024)S(1)} %pad_clamp_fusion.2), kind=kCustom, calls=%fused_computation.1.clone | custom fusion | bytes 25165920 | tf_op jit(solution)/shard_map/jit(_take)/gather | solution.py:30
  59.7 83.6 %all-to-all-done = bf16[16,256,1024]{2,1,0:T(8,128)(2,1)} async-done(((bf16[16,256,1024]{2,1,0:T(8,128)(2,1)}), bf16[16,256,1024]{2,1,0:T(8,128)(2,1)}, u32[]{:S(2)}, u32[]{:S(2)}) %all-to-all-start) | async-done | bytes 8388640 | tf_op jit(solution)/shard_map/all_to_all | solution.py:21
  143.4 0.0 copy-done.2
  143.4 8.6 %pad_maximum_fusion.1 = bf16[20,256,1024]{2,1,0:T(8,128)(2,1)} fusion(bf16[16,256,1024]{2,1,0:T(8,128)(2,1)} %all-to-all-done, bf16[4,256,1024]{2,1,0:T(8,128)(2,1)S(1)} %bitcast.26), kind=kLoop, calls=%fused_computation.12 | loop fusion | flops 5242880 | bytes 20971520 | tf_op jit(solution)/shard_map/concatenate | solution.py:22
  152.0 10.1 %gather_fusion.1 = bf16[24,256,1024]{2,1,0:T(8,128)(2,1)} fusion(bf16[20,256,1024]{2,1,0:T(8,128)(2,1)} %pad_maximum_fusion.1, s32[1024]{0:T(1024)S(1)} %pad_clamp_fusion), kind=kCustom, calls=%fused_computation.3 | custom fusion | bytes 25165920 | tf_op jit(solution)/shard_map/jit(_take)/gather | solution.py:31
  162.1 13.1 %fusion.8 = f32[1,24,256,256]{3,2,1,0:T(8,128)} fusion(bf16[24,256,1024]{2,1,0:T(8,128)(2,1)} %gather_fusion.1, pred[24]{0:T(512)(128)(4,1)S(1)} %get-tuple-element.8, bf16[24,256,1024]{2,1,0:T(8,128)(2,1)} %gather_fusion.2, pred[24]{0:T(512)(128)(4,1)S(1)} %get-tuple-element.6), kind=kOutput, calls=%fused_computation.16 | convolution fusion | flops 3233808384 | bytes 31457328 | tf_op jit(solution)/shard_map/tak,tbk->tab/dot_general | solution.py:32
  175.1 13.0 %fusion.11 = f32[1,24,256,256]{3,2,1,0:T(8,128)} fusion(bf16[24,256,1024]{2,1,0:T(8,128)(2,1)} %gather_fusion.1, pred[24]{0:T(512)(128)(4,1)S(1)} %get-tuple-element.8, bf16[24,256,1024]{2,1,0:T(8,128)(2,1)} %gather_fusion.3, pred[24]{0:T(512)(128)(4,1)S(1)} %get-tuple-element.6), kind=kOutput, calls=%fused_computation.17 | convolution fusion | flops 3233808384 | bytes 31457328 | tf_op jit(solution)/shard_map/tak,tbk->tab/dot_general | solution.py:33
  188.2 10.5 %pad_maximum_fusion = f32[2,24,256,256]{3,2,1,0:T(8,128)} fusion(f32[1,24,256,256]{3,2,1,0:T(8,128)} %fusion.11, f32[1,24,256,256]{3,2,1,0:T(8,128)} %fusion.8), kind=kLoop, calls=%fused_computation.4 | loop fusion | flops 3145728 | bytes 25165824 | tf_op jit(solution)/shard_map/stack | solution.py:34
  198.7 0.0 all-gather.4.cloned.1.call-update
  198.7 445.7 %all-gather.4.cloned.1.call-done = f32[16,24,256,256]{3,2,1,0:T(8,128)} async-done(((f32[2,24,256,256]{3,2,1,0:T(8,128)}), f32[16,24,256,256]{3,2,1,0:T(8,128)}) %all-gather.4.cloned.1.call-update) | async-done | bytes 100663312 | tf_op jit(solution)/shard_map/all_gather | solution.py:35
  644.4 0.0 copy-start.1
  644.4 35.9 %reduce_sum.9 = f32[2,24,256,256]{3,2,1,0:T(8,128)} reduce(f32[8,2,24,256,256]{4,3,2,1,0:T(8,128)} %bitcast.11, f32[]{:T(128)} %constant.78.clone.1), dimensions={0}, to_apply=%region_2.4 | reduce | flops 22020096 | bytes 113246208 | tf_op jit(solution)/shard_map/reduce_sum | solution.py:35
  680.3 2.4 fusion.14
  682.7 0.0 copy-done.1
  (9 shorter events, 0.1 us)
Async XLA Ops:
  6.5 39.4 %copy-start = (bf16[1024,1024]{1,0:T(8,128)(2,1)S(1)}, bf16[1024,1024]{1,0:T(8,128)(2,1)}, u32[]{:S(2)}) copy-start(bf16[1024,1024]{1,0:T(8,128)(2,1)} %param.6) | copy-start | bytes 6291460
  40.9 5.0 copy-start.3
  40.9 102.5 %all-to-all-start = ((bf16[16,256,1024]{2,1,0:T(8,128)(2,1)}), bf16[16,256,1024]{2,1,0:T(8,128)(2,1)}, u32[]{:S(2)}, u32[]{:S(2)}) async-start(bf16[16,256,1024]{2,1,0:T(8,128)(2,1)} %broadcast_select_fusion.1), calls=%async_computation | async-start | bytes 16777216 | tf_op jit(solution)/shard_map/all_to_all | solution.py:21
  45.8 598.6 %all-gather.4.cloned.1.call-start = ((), (), s32[]{:S(2)}) async-start(), calls=%async_computation.1 | async-start | bytes 113246208 | tf_op jit(solution)/shard_map/all_gather | solution.py:35
  51.9 91.5 %copy-start.2 = (bf16[1024,1024]{1,0:T(8,128)(2,1)S(1)}, bf16[1024,1024]{1,0:T(8,128)(2,1)}, u32[]{:S(2)}) copy-start(bf16[1024,1024]{1,0:T(8,128)(2,1)} %param.8) | copy-start | bytes 6291460
  644.4 38.3 %copy-start.1 = (bf16[1024,1024]{1,0:T(8,128)(2,1)S(1)}, bf16[1024,1024]{1,0:T(8,128)(2,1)}, u32[]{:S(2)}) copy-start(bf16[1024,1024]{1,0:T(8,128)(2,1)} %param.6) | copy-start | bytes 6291460
Sparse Core Ops, SparseCore 0:
  198.9 445.5 all-gather.3
